TPU v7x, 32 devices: a whole 2x2x4 slice. The times are simulated.
32 devices in a mesh: ctx: 16 (over z, x, core), chan: 2 (over y).
Axes of the slice: x: 2, y: 2, z: 4, core: 2. Of those that a mesh axis runs over, the one named last changes fastest.
Arguments:
- query_act: bfloat16 [2048, 1024], P('ctx', 'chan'), may hold values from -6 to 6
- key_act: bfloat16 [2048, 1024], P('ctx', 'chan'), may hold values from -6 to 6
- value_act: bfloat16 [2048, 1024], P('ctx', 'chan'), may hold values from -6 to 6
- filters: bfloat16 [2048, 1024], P('ctx', 'chan'), may hold values from -0.125 to 0.125
- skip_scale: float32 [1024], P('chan'), may hold values from -4 to 4
- w_out: bfloat16 [1024, 4096], P('chan'), may hold values from -0.25 to 0.25
Outputs:
- projected: bfloat16 [2048, 4096], P('ctx', 'chan')
All inputs are finite; a program needn't handle non-finite values.
Results may differ from a plain program's by a relative error of at most 0.015.
Values may be sent and summed in bfloat16 or wider, within the bound.
A program may use at most 64 MiB of HBM per device.

v0:
```python
import math
import jax
import jax.numpy as jnp
from jax import lax
from jax.sharding import PartitionSpec as P

precise = lax.Precision.HIGHEST


def phase_table(row_count, col_count, modulus, factor):
    row_index = lax.broadcasted_iota(jnp.int32, (row_count, col_count), 0)
    col_index = lax.broadcasted_iota(jnp.int32, (row_count, col_count), 1)
    phase_angle = (row_index * col_index % modulus).astype(jnp.float32) * (2.0 * math.pi / modulus)
    return (jnp.cos(phase_angle) * factor, jnp.sin(phase_angle) * factor)


def twiddle(freq_index, pos_index, modulus):
    phase_angle = (freq_index * pos_index % modulus).astype(jnp.float32) * (2.0 * math.pi / modulus)
    return (jnp.cos(phase_angle), jnp.sin(phase_angle))


def shards(query_act, key_act, value_act, filters, skip_scale, w_out):
    tok_rows, chan_width = key_act.shape
    ctx_size = lax.axis_size("ctx")
    per_dev = tok_rows // ctx_size
    fft_length = 2 * tok_rows * ctx_size
    freq_blocks = 2 * ctx_size
    ctx_index = lax.axis_index("ctx")
    gated_in = (key_act.astype(jnp.float32) * value_act.astype(jnp.float32)).astype(jnp.bfloat16)
    sent_input, sent_filter = (
        lax.all_to_all(
            gated_in.reshape(1, ctx_size, per_dev, chan_width),
            "ctx",
            split_axis=1,
            concat_axis=0,
            tiled=True,
        ),
        lax.all_to_all(
            filters.reshape(1, ctx_size, per_dev, chan_width),
            "ctx",
            split_axis=1,
            concat_axis=0,
            tiled=True,
        ),
    )
    block_cos, block_sin = phase_table(freq_blocks, ctx_size, freq_blocks, 1.0)
    offsets = ctx_index * per_dev + lax.broadcasted_iota(jnp.int32, (1, per_dev), 1)
    all_freq = lax.broadcasted_iota(jnp.int32, (freq_blocks, 1), 0)
    front_cos, front_sin = twiddle(all_freq, offsets, fft_length)
    front_cos = front_cos[:, :, None]
    front_sin = front_sin[:, :, None]

    def first_section(signal):
        values32 = signal.reshape(ctx_size, per_dev, chan_width).astype(jnp.float32)
        real_part = jnp.einsum("kp,pjc->kjc", block_cos, values32, precision=precise)
        imag_part = -jnp.einsum("kp,pjc->kjc", block_sin, values32, precision=precise)
        out_real = real_part * front_cos + imag_part * front_sin
        out_imag = imag_part * front_cos - real_part * front_sin
        return jnp.stack([out_real, out_imag]).reshape(2, ctx_size, 2, per_dev, chan_width)

    cycle_cos, cycle_sin = phase_table(tok_rows, tok_rows, tok_rows, 1.0)

    def cycle_apply(table, operand):
        return jnp.einsum("kn,zmnc->zmkc", table, operand, precision=precise)

    spec_input = lax.all_to_all(
        first_section(sent_input), "ctx", split_axis=1, concat_axis=3, tiled=True
    )
    spec_filter = lax.all_to_all(
        first_section(sent_filter), "ctx", split_axis=1, concat_axis=3, tiled=True
    )

    def forward(portion):
        real_in = portion[0]
        imag_in = portion[1]
        out_real = cycle_apply(cycle_cos, real_in) + cycle_apply(cycle_sin, imag_in)
        out_imag = cycle_apply(cycle_cos, imag_in) - cycle_apply(cycle_sin, real_in)
        return (out_real, out_imag)

    input_real, input_imag = forward(spec_input)
    filter_real, filter_imag = forward(spec_filter)
    prod_real = input_real * filter_real - input_imag * filter_imag
    prod_imag = input_real * filter_imag + input_imag * filter_real
    back_real = cycle_apply(cycle_cos, prod_real) - cycle_apply(cycle_sin, prod_imag)
    back_imag = cycle_apply(cycle_cos, prod_imag) + cycle_apply(cycle_sin, prod_real)
    mixed = jnp.stack([back_real, back_imag])
    inverted = mixed[:, 0]
    pack_width = inverted.shape[-1]
    own_freq = 2 * ctx_index + lax.broadcasted_iota(jnp.int32, (2, 1), 0)
    all_offsets = lax.broadcasted_iota(jnp.int32, (1, tok_rows), 1)
    back_cos, back_sin = twiddle(own_freq, all_offsets, fft_length)
    back_cos = back_cos[:, :, None]
    back_sin = back_sin[:, :, None]
    turned_real = inverted[0] * back_cos - inverted[1] * back_sin
    turned_imag = inverted[0] * back_sin + inverted[1] * back_cos
    turned = jnp.stack([turned_real, turned_imag]).reshape(2, 2, ctx_size, per_dev, pack_width)
    last_cos, last_sin = phase_table(ctx_size, freq_blocks, freq_blocks, 1.0 / fft_length)

    def last_apply(table, operand):
        return jnp.einsum("nk,kzmc->nzmc", table, operand, precision=precise)

    portion = lax.all_to_all(turned, "ctx", split_axis=2, concat_axis=1, tiled=True)
    returned = last_apply(last_cos, portion[0]) - last_apply(last_sin, portion[1])
    convolved = lax.all_to_all(returned, "ctx", split_axis=0, concat_axis=1, tiled=True).reshape(
        tok_rows, chan_width
    )
    gated = (
        query_act.astype(jnp.float32)
        * (convolved + skip_scale[None, :] * gated_in.astype(jnp.float32))
    ).astype(jnp.bfloat16)
    summed = lax.psum_scatter(
        lax.dot_general(
            w_out, gated, (((0,), (1,)), ((), ())), preferred_element_type=jnp.float32
        ).astype(jnp.bfloat16),
        "chan",
        scatter_dimension=0,
        tiled=True,
    )
    return summed.T


def solution(mesh):
    return jax.shard_map(
        shards,
        mesh=mesh,
        in_specs=(
            P("ctx", "chan"),
            P("ctx", "chan"),
            P("ctx", "chan"),
            P("ctx", "chan"),
            P("chan"),
            P("chan", None),
        ),
        out_specs=P("ctx", "chan"),
        check_vma=False,
    )
```

profile of v0, /device:TPU:0, one launch (start us, length us, event | category | flops | bytes accessed | tf_op | source)
XLA Modules:
  0.0 180.7 jit_solution(6431051070737040364)
XLA Ops:
  6.5 1.7 fusion.49
  8.2 7.4 %all-to-all-start = ((bf16[1,16,8,512]{3,2,0,1:T(8,128)(2,1)}), bf16[1,16,8,512]{3,2,0,1:T(8,128)(2,1)S(1)}, u32[]{:S(2)}, u32[]{:S(2)}) async-start(bf16[1,16,8,512]{3,2,0,1:T(8,128)(2,1)} %fusion.49), calls=%async_computation | async-start | bytes 262144 | tf_op jit(solution)/shard_map/all_to_all | solution.py:31
  15.6 0.1 fusion.103
  15.7 7.8 %all-to-all-done = bf16[1,16,8,512]{3,2,0,1:T(8,128)(2,1)S(1)} async-done(((bf16[1,16,8,512]{3,2,0,1:T(8,128)(2,1)}), bf16[1,16,8,512]{3,2,0,1:T(8,128)(2,1)S(1)}, u32[]{:S(2)}, u32[]{:S(2)}) %all-to-all-start) | async-done | bytes 131104 | tf_op jit(solution)/shard_map/all_to_all | solution.py:31
  23.5 3.5 %all-to-all-start.2 = ((bf16[1,16,8,512]{3,2,0,1:T(8,128)(2,1)}), bf16[1,16,8,512]{3,2,0,1:T(8,128)(2,1)S(1)}, u32[]{:S(2)}, u32[]{:S(2)}) async-start(bf16[1,16,8,512]{3,2,0,1:T(8,128)(2,1)} %bitcast.166), calls=%async_computation.2 | async-start | bytes 262144 | tf_op jit(solution)/shard_map/all_to_all | solution.py:38
  27.0 0.5 convolution_negate_fusion.1
  27.5 0.5 fusion.24
  28.0 6.9 %all-to-all-done.2 = bf16[1,16,8,512]{3,2,0,1:T(8,128)(2,1)S(1)} async-done(((bf16[1,16,8,512]{3,2,0,1:T(8,128)(2,1)}), bf16[1,16,8,512]{3,2,0,1:T(8,128)(2,1)S(1)}, u32[]{:S(2)}, u32[]{:S(2)}) %all-to-all-start.2) | async-done | bytes 131104 | tf_op jit(solution)/shard_map/all_to_all | solution.py:38
  34.9 0.5 fusion.21
  35.4 0.6 multiply_add_fusion.1
  36.0 0.3 copy.79
  36.4 0.3 copy.80
  36.7 1.1 pad_maximum_fusion.1
  37.8 3.7 %all-to-all-start.3 = ((f32[2,16,2,8,512]{4,3,2,0,1:T(8,128)}), f32[2,16,2,8,512]{4,3,2,0,1:T(8,128)S(1)}, u32[]{:S(2)}, u32[]{:S(2)}) async-start(f32[2,16,2,8,512]{4,3,2,0,1:T(8,128)} %pad_maximum_fusion.1), calls=%async_computation.3 | async-start | bytes 2097152 | tf_op jit(solution)/shard_map/all_to_all | solution.py:69
  41.4 0.3 copy.78
  41.7 0.3 copy.77
  42.1 1.1 pad_maximum_fusion
  43.1 21.2 %all-to-all-done.3 = f32[2,16,2,8,512]{4,3,2,0,1:T(8,128)S(1)} async-done(((f32[2,16,2,8,512]{4,3,2,0,1:T(8,128)}), f32[2,16,2,8,512]{4,3,2,0,1:T(8,128)S(1)}, u32[]{:S(2)}, u32[]{:S(2)}) %all-to-all-start.3) | async-done | bytes 1048608 | tf_op jit(solution)/shard_map/all_to_all | solution.py:69
  64.3 6.8 %all-to-all-start.1 = ((f32[2,16,2,8,512]{4,3,2,0,1:T(8,128)}), f32[2,16,2,8,512]{4,3,2,0,1:T(8,128)S(1)}, u32[]{:S(2)}, u32[]{:S(2)}) async-start(f32[2,16,2,8,512]{4,3,2,0,1:T(8,128)} %pad_maximum_fusion), calls=%async_computation.1 | async-start | bytes 2097152 | tf_op jit(solution)/shard_map/all_to_all | solution.py:66
  71.1 0.2 reduce-scatter.2.cloned.1.call-start
  71.4 0.1 fusion.108
  71.5 0.1 copy.108
  71.6 1.1 fusion.16
  72.7 1.1 fusion.15
  73.8 20.2 %all-to-all-done.1 = f32[2,16,2,8,512]{4,3,2,0,1:T(8,128)S(1)} async-done(((f32[2,16,2,8,512]{4,3,2,0,1:T(8,128)}), f32[2,16,2,8,512]{4,3,2,0,1:T(8,128)S(1)}, u32[]{:S(2)}, u32[]{:S(2)}) %all-to-all-start.1) | async-done | bytes 1048608 | tf_op jit(solution)/shard_map/all_to_all | solution.py:66
  94.1 0.1 copy.109
  94.2 1.1 fusion.14
  95.3 1.1 fusion.13
  96.4 1.1 convolution_subtract_fusion.1
  97.5 1.1 convolution_add_fusion.1
  98.7 1.1 convolution_add_fusion.2
  99.8 1.1 multiply_subtract_fusion
  100.9 0.9 fusion.8
  101.8 0.9 fusion.10
  102.7 0.9 fusion.1
  103.6 1.2 subtract_bitcast_fusion
  104.8 0.1 pad_maximum_fusion.2
  104.9 0.0 copy-start.1
  105.0 0.1 copy.81
  105.1 31.8 %all_to_all.72 = f32[2,2,16,8,512]{4,3,1,0,2:T(8,128)S(1)} all-to-all(f32[2,2,16,8,512]{4,3,1,0,2:T(8,128)S(1)} %copy.81), channel_id=1, replica_groups=mesh['ctx'=16,'chan'=2] {'ctx'}, dimensions={2} | all-to-all | bytes 2097152 | tf_op jit(solution)/shard_map/all_to_all | solution.py:102
  136.8 0.1 fusion.183
  136.9 0.7 fusion.5
  137.6 0.7 fusion.3
  138.3 0.2 copy.64
  138.5 14.8 %all_to_all.73 = f32[16,1,8,512]{3,2,1,0:T(8,128)S(1)} all-to-all(f32[16,1,8,512]{3,2,1,0:T(8,128)S(1)} %copy.64), channel_id=1, replica_groups=mesh['ctx'=16,'chan'=2] {'ctx'}, dimensions={0} | all-to-all | bytes 524288 | tf_op jit(solution)/shard_map/all_to_all | solution.py:104
  153.3 1.7 fusion
  155.0 0.0 reduce-scatter.2.cloned.1.call-update
  155.1 18.8 %reduce-scatter.2.cloned.1.call-done = bf16[2048,128]{0,1:T(8,128)(2,1)} async-done(((bf16[4096,128]{0,1:T(8,128)(2,1)}), bf16[2048,128]{0,1:T(8,128)(2,1)}) %reduce-scatter.2.cloned.1.call-update) | async-done | bytes 524304 | tf_op jit(solution)/shard_map/reduce_scatter | solution.py:111
  (11 shorter events, 0.0 us)
Async XLA Ops:
  8.2 15.3 %all-to-all-start = ((bf16[1,16,8,512]{3,2,0,1:T(8,128)(2,1)}), bf16[1,16,8,512]{3,2,0,1:T(8,128)(2,1)S(1)}, u32[]{:S(2)}, u32[]{:S(2)}) async-start(bf16[1,16,8,512]{3,2,0,1:T(8,128)(2,1)} %fusion.49), calls=%async_computation | async-start | bytes 262144 | tf_op jit(solution)/shard_map/all_to_all | solution.py:31
  23.5 11.4 %all-to-all-start.2 = ((bf16[1,16,8,512]{3,2,0,1:T(8,128)(2,1)}), bf16[1,16,8,512]{3,2,0,1:T(8,128)(2,1)S(1)}, u32[]{:S(2)}, u32[]{:S(2)}) async-start(bf16[1,16,8,512]{3,2,0,1:T(8,128)(2,1)} %bitcast.166), calls=%async_computation.2 | async-start | bytes 262144 | tf_op jit(solution)/shard_map/all_to_all | solution.py:38
  37.8 26.6 %all-to-all-start.3 = ((f32[2,16,2,8,512]{4,3,2,0,1:T(8,128)}), f32[2,16,2,8,512]{4,3,2,0,1:T(8,128)S(1)}, u32[]{:S(2)}, u32[]{:S(2)}) async-start(f32[2,16,2,8,512]{4,3,2,0,1:T(8,128)} %pad_maximum_fusion.1), calls=%async_computation.3 | async-start | bytes 2097152 | tf_op jit(solution)/shard_map/all_to_all | solution.py:69
  64.3 29.8 %all-to-all-start.1 = ((f32[2,16,2,8,512]{4,3,2,0,1:T(8,128)}), f32[2,16,2,8,512]{4,3,2,0,1:T(8,128)S(1)}, u32[]{:S(2)}, u32[]{:S(2)}) async-start(f32[2,16,2,8,512]{4,3,2,0,1:T(8,128)} %pad_maximum_fusion), calls=%async_computation.1 | async-start | bytes 2097152 | tf_op jit(solution)/shard_map/all_to_all | solution.py:66
  71.1 102.7 %reduce-scatter.2.cloned.1.call-start = ((), (), s32[]{:S(2)}) async-start(), calls=%async_computation.7 | async-start | bytes 1572864 | tf_op jit(solution)/shard_map/reduce_scatter | solution.py:111
  104.9 48.4 %copy-start = (bf16[512,4096]{1,0:T(8,128)(2,1)S(1)}, bf16[512,4096]{1,0:T(8,128)(2,1)}, u32[]{:S(2)}) copy-start(bf16[512,4096]{1,0:T(8,128)(2,1)} %param.11) | copy-start | bytes 12582916
  104.9 48.4 %copy-start.1 = (bf16[128,512]{1,0:T(8,128)(2,1)S(1)}, bf16[128,512]{1,0:T(8,128)(2,1)}, u32[]{:S(2)}) copy-start(bf16[128,512]{1,0:T(8,128)(2,1)} %param.8) | copy-start | bytes 393220
  104.9 48.4 %copy-start.2 = (bf16[128,512]{1,0:T(8,128)(2,1)S(1)}, bf16[128,512]{1,0:T(8,128)(2,1)}, u32[]{:S(2)}) copy-start(bf16[128,512]{1,0:T(8,128)(2,1)} %param.7) | copy-start | bytes 393220
  104.9 48.4 %copy-start.3 = (bf16[128,512]{1,0:T(8,128)(2,1)S(1)}, bf16[128,512]{1,0:T(8,128)(2,1)}, u32[]{:S(2)}) copy-start(bf16[128,512]{1,0:T(8,128)(2,1)} %param.6) | copy-start | bytes 393220
  105.0 48.4 %copy-start.4 = (f32[512]{0:T(512)S(1)}, f32[512]{0:T(512)}, u32[]{:S(2)}) copy-start(f32[512]{0:T(512)} %param.10) | copy-start | bytes 6148
Sparse Core Ops, SparseCore 0:
  155.2 18.6 reduce-scatter.1
where the time goes:
time: 181 us
  waiting for transfers between devices  75 us (41%)
  blocking collectives  46.6 us (26%)
  starting transfers between devices  21.6 us (12%)
  matrix products  17.9 us (10%)
  between operations  13.7 us (8%)
  other arithmetic  4.15 us (2%)
    all_to_all x1, blocking collectives, shards(): lax.all_to_all(turned, 'ctx', split_axis=2, concat_axis=1, tiled=True)  31.8 us
    all_to_all x1, waiting for transfers between devices, shards(): lax.all_to_all(first_section(sent_filter), 'ctx', split_axis=1, concat_ax...  21.2 us
    all_to_all x1, waiting for transfers between devices, shards(): lax.all_to_all(first_section(sent_input), 'ctx', split_axis=1, concat_axi...  20.2 us
    reduce_scatter x1, waiting for transfers between devices, shards(): lax.psum_scatter(lax.dot_general(w_out, gated, (((0,), (1,)), ((), ())),...  18.8 us
    all_to_all x1, blocking collectives, shards(): lax.all_to_all(returned, 'ctx', split_axis=0, concat_axis=1, tiled=True)  14.8 us
    dot_general x12, matrix products, cycle_apply(): return jnp.einsum('kn,zmnc->zmkc', table, operand, precision=precise)  12.8 us
    all_to_all x1, waiting for transfers between devices, shards(): lax.all_to_all(gated_in.reshape(1, ctx_size, per_dev, chan_width), 'ctx',...  7.8 us
    all_to_all x1, starting transfers between devices, shards(): lax.all_to_all(gated_in.reshape(1, ctx_size, per_dev, chan_width), 'ctx',...  7.36 us
  transfers between devices with their start and end apart: 5, of which 5 were waited for; matrix products, arithmetic and copies ran while one was open for 3% of the time, Pallas kernels for 0%

commit v1 on v0

--- a/solution.py
+++ b/solution.py
@@ -1,3 +1,4 @@
+import functools
 import math
 import jax
 import jax.numpy as jnp
@@ -5,6 +6,17 @@
 from jax.sharding import PartitionSpec as P
 
 precise = lax.Precision.HIGHEST
+
+
+def step_on_regions_for(inp, ax_name):
+    s_next = jax.lax.psum(1, ax_name)
+    back = jnp.split(inp, s_next, axis=2)
+    lower = jnp.stack(back, axis=0)
+    field_out = jax.lax.all_to_all(lower, ax_name, 0, 0)
+    return jnp.concatenate(field_out, axis=1)
+
+
+fit_the_sums_all = functools.partial(step_on_regions_for, ax_name="ctx")
 
 
 def phase_table(row_count, col_count, modulus, factor):
@@ -99,7 +111,7 @@
     def last_apply(table, operand):
         return jnp.einsum("nk,kzmc->nzmc", table, operand, precision=precise)
 
-    portion = lax.all_to_all(turned, "ctx", split_axis=2, concat_axis=1, tiled=True)
+    portion = fit_the_sums_all(turned)
     returned = last_apply(last_cos, portion[0]) - last_apply(last_sin, portion[1])
     convolved = lax.all_to_all(returned, "ctx", split_axis=0, concat_axis=1, tiled=True).reshape(
         tok_rows, chan_width

time: 181 us -> 181 us (level)
  no operation moved by 1% of the time
where the time goes in v1:
time: 181 us
  waiting for transfers between devices  74.9 us (41%)
  blocking collectives  46.6 us (26%)
  starting transfers between devices  21.6 us (12%)
  matrix products  17.9 us (10%)
  between operations  13.8 us (8%)
  other arithmetic  4.2 us (2%)
    all_to_all x1, blocking collectives, step_on_regions_for(): field_out = jax.lax.all_to_all(lower, ax_name, 0, 0)  31.8 us
    all_to_all x1, waiting for transfers between devices, shards(): lax.all_to_all(first_section(sent_filter), 'ctx', split_axis=1, concat_ax...  21.2 us
    all_to_all x1, waiting for transfers between devices, shards(): lax.all_to_all(first_section(sent_input), 'ctx', split_axis=1, concat_axi...  20.2 us
    reduce_scatter x1, waiting for transfers between devices, shards(): lax.psum_scatter(lax.dot_general(w_out, gated, (((0,), (1,)), ((), ())),...  18.8 us
    all_to_all x1, blocking collectives, shards(): lax.all_to_all(returned, 'ctx', split_axis=0, concat_axis=1, tiled=True)  14.8 us
    dot_general x12, matrix products, cycle_apply(): return jnp.einsum('kn,zmnc->zmkc', table, operand, precision=precise)  12.8 us
    all_to_all x1, waiting for transfers between devices, shards(): lax.all_to_all(gated_in.reshape(1, ctx_size, per_dev, chan_width), 'ctx',...  7.8 us
    all_to_all x1, starting transfers between devices, shards(): lax.all_to_all(gated_in.reshape(1, ctx_size, per_dev, chan_width), 'ctx',...  7.36 us
  transfers between devices with their start and end apart: 5, of which 5 were waited for; matrix products, arithmetic and copies ran while one was open for 3% of the time, Pallas kernels for 0%

profile of v1, /device:TPU:0, one launch (start us, length us, event | category | flops | bytes accessed | tf_op | source)
XLA Modules:
  0.0 180.8 jit_solution(16473921402815745993)
XLA Ops:
  6.5 1.7 fusion.66
  8.2 7.4 %all-to-all-start = ((bf16[1,16,8,512]{3,2,0,1:T(8,128)(2,1)}), bf16[1,16,8,512]{3,2,0,1:T(8,128)(2,1)S(1)}, u32[]{:S(2)}, u32[]{:S(2)}) async-start(bf16[1,16,8,512]{3,2,0,1:T(8,128)(2,1)} %fusion.66), calls=%async_computation | async-start | bytes 262144 | tf_op jit(solution)/shard_map/all_to_all | solution.py:43
  15.6 0.1 fusion.120
  15.7 7.8 %all-to-all-done = bf16[1,16,8,512]{3,2,0,1:T(8,128)(2,1)S(1)} async-done(((bf16[1,16,8,512]{3,2,0,1:T(8,128)(2,1)}), bf16[1,16,8,512]{3,2,0,1:T(8,128)(2,1)S(1)}, u32[]{:S(2)}, u32[]{:S(2)}) %all-to-all-start) | async-done | bytes 131104 | tf_op jit(solution)/shard_map/all_to_all | solution.py:43
  23.5 3.5 %all-to-all-start.2 = ((bf16[1,16,8,512]{3,2,0,1:T(8,128)(2,1)}), bf16[1,16,8,512]{3,2,0,1:T(8,128)(2,1)S(1)}, u32[]{:S(2)}, u32[]{:S(2)}) async-start(bf16[1,16,8,512]{3,2,0,1:T(8,128)(2,1)} %bitcast.228), calls=%async_computation.2 | async-start | bytes 262144 | tf_op jit(solution)/shard_map/all_to_all | solution.py:50
  27.0 0.5 convolution_negate_fusion.1
  27.5 0.5 fusion.24
  28.0 6.9 %all-to-all-done.2 = bf16[1,16,8,512]{3,2,0,1:T(8,128)(2,1)S(1)} async-done(((bf16[1,16,8,512]{3,2,0,1:T(8,128)(2,1)}), bf16[1,16,8,512]{3,2,0,1:T(8,128)(2,1)S(1)}, u32[]{:S(2)}, u32[]{:S(2)}) %all-to-all-start.2) | async-done | bytes 131104 | tf_op jit(solution)/shard_map/all_to_all | solution.py:50
  34.9 0.5 fusion.21
  35.4 0.6 multiply_add_fusion.1
  36.0 0.3 copy.122
  36.4 0.3 copy.123
  36.7 1.1 pad_maximum_fusion.1
  37.8 3.7 %all-to-all-start.3 = ((f32[2,16,2,8,512]{4,3,2,0,1:T(8,128)}), f32[2,16,2,8,512]{4,3,2,0,1:T(8,128)S(1)}, u32[]{:S(2)}, u32[]{:S(2)}) async-start(f32[2,16,2,8,512]{4,3,2,0,1:T(8,128)} %pad_maximum_fusion.1), calls=%async_computation.3 | async-start | bytes 2097152 | tf_op jit(solution)/shard_map/all_to_all | solution.py:81
  41.4 0.3 copy.121
  41.7 0.3 copy.120
  42.1 1.1 pad_maximum_fusion
  43.1 21.2 %all-to-all-done.3 = f32[2,16,2,8,512]{4,3,2,0,1:T(8,128)S(1)} async-done(((f32[2,16,2,8,512]{4,3,2,0,1:T(8,128)}), f32[2,16,2,8,512]{4,3,2,0,1:T(8,128)S(1)}, u32[]{:S(2)}, u32[]{:S(2)}) %all-to-all-start.3) | async-done | bytes 1048608 | tf_op jit(solution)/shard_map/all_to_all | solution.py:81
  64.3 6.8 %all-to-all-start.1 = ((f32[2,16,2,8,512]{4,3,2,0,1:T(8,128)}), f32[2,16,2,8,512]{4,3,2,0,1:T(8,128)S(1)}, u32[]{:S(2)}, u32[]{:S(2)}) async-start(f32[2,16,2,8,512]{4,3,2,0,1:T(8,128)} %pad_maximum_fusion), calls=%async_computation.1 | async-start | bytes 2097152 | tf_op jit(solution)/shard_map/all_to_all | solution.py:78
  71.1 0.2 reduce-scatter.2.cloned.1.call-start
  71.4 0.1 fusion.125
  71.5 0.1 copy.165
  71.6 1.1 fusion.16
  72.7 1.1 fusion.15
  73.8 20.2 %all-to-all-done.1 = f32[2,16,2,8,512]{4,3,2,0,1:T(8,128)S(1)} async-done(((f32[2,16,2,8,512]{4,3,2,0,1:T(8,128)}), f32[2,16,2,8,512]{4,3,2,0,1:T(8,128)S(1)}, u32[]{:S(2)}, u32[]{:S(2)}) %all-to-all-start.1) | async-done | bytes 1048608 | tf_op jit(solution)/shard_map/all_to_all | solution.py:78
  94.1 0.1 copy.166
  94.2 1.1 fusion.14
  95.3 1.1 fusion.13
  96.4 1.1 convolution_subtract_fusion.1
  97.5 1.1 convolution_add_fusion.1
  98.7 1.1 convolution_add_fusion.2
  99.8 1.1 multiply_subtract_fusion
  100.9 0.9 fusion.8
  101.8 0.9 fusion.10
  102.7 0.9 fusion.1
  103.6 1.2 subtract_bitcast_fusion
  105.1 0.0 copy-start
  105.1 0.0 copy-start.1
  105.1 0.0 copy-start.2
  105.1 31.8 %all_to_all.62 = f32[16,2,2,1,8,512]{5,4,2,1,3,0:T(8,128)S(1)} all-to-all(f32[16,2,2,1,8,512]{5,4,2,1,3,0:T(8,128)S(1)} %fusion.50), channel_id=1, replica_groups=mesh['ctx'=16,'chan'=2] {'ctx'}, dimensions={0} | all-to-all | bytes 2097152 | tf_op jit(solution)/shard_map/all_to_all | solution.py:15
  136.9 0.1 fusion.200
  137.0 0.7 fusion.5
  137.7 0.7 fusion.3
  138.4 0.2 copy.107
  138.5 14.8 %all_to_all.63 = f32[16,1,8,512]{3,2,1,0:T(8,128)S(1)} all-to-all(f32[16,1,8,512]{3,2,1,0:T(8,128)S(1)} %copy.107), channel_id=1, replica_groups=mesh['ctx'=16,'chan'=2] {'ctx'}, dimensions={0} | all-to-all | bytes 524288 | tf_op jit(solution)/shard_map/all_to_all | solution.py:116
  153.4 1.7 fusion
  155.1 0.0 reduce-scatter.2.cloned.1.call-update
  155.1 18.8 %reduce-scatter.2.cloned.1.call-done = bf16[2048,128]{0,1:T(8,128)(2,1)} async-done(((bf16[4096,128]{0,1:T(8,128)(2,1)}), bf16[2048,128]{0,1:T(8,128)(2,1)}) %reduce-scatter.2.cloned.1.call-update) | async-done | bytes 524304 | tf_op jit(solution)/shard_map/reduce_scatter | solution.py:123
  (25 shorter events, 0.1 us)
Async XLA Ops:
  8.2 15.3 %all-to-all-start = ((bf16[1,16,8,512]{3,2,0,1:T(8,128)(2,1)}), bf16[1,16,8,512]{3,2,0,1:T(8,128)(2,1)S(1)}, u32[]{:S(2)}, u32[]{:S(2)}) async-start(bf16[1,16,8,512]{3,2,0,1:T(8,128)(2,1)} %fusion.66), calls=%async_computation | async-start | bytes 262144 | tf_op jit(solution)/shard_map/all_to_all | solution.py:43
  23.5 11.4 %all-to-all-start.2 = ((bf16[1,16,8,512]{3,2,0,1:T(8,128)(2,1)}), bf16[1,16,8,512]{3,2,0,1:T(8,128)(2,1)S(1)}, u32[]{:S(2)}, u32[]{:S(2)}) async-start(bf16[1,16,8,512]{3,2,0,1:T(8,128)(2,1)} %bitcast.228), calls=%async_computation.2 | async-start | bytes 262144 | tf_op jit(solution)/shard_map/all_to_all | solution.py:50
  37.8 26.6 %all-to-all-start.3 = ((f32[2,16,2,8,512]{4,3,2,0,1:T(8,128)}), f32[2,16,2,8,512]{4,3,2,0,1:T(8,128)S(1)}, u32[]{:S(2)}, u32[]{:S(2)}) async-start(f32[2,16,2,8,512]{4,3,2,0,1:T(8,128)} %pad_maximum_fusion.1), calls=%async_computation.3 | async-start | bytes 2097152 | tf_op jit(solution)/shard_map/all_to_all | solution.py:81
  64.3 29.8 %all-to-all-start.1 = ((f32[2,16,2,8,512]{4,3,2,0,1:T(8,128)}), f32[2,16,2,8,512]{4,3,2,0,1:T(8,128)S(1)}, u32[]{:S(2)}, u32[]{:S(2)}) async-start(f32[2,16,2,8,512]{4,3,2,0,1:T(8,128)} %pad_maximum_fusion), calls=%async_computation.1 | async-start | bytes 2097152 | tf_op jit(solution)/shard_map/all_to_all | solution.py:78
  71.1 102.8 %reduce-scatter.2.cloned.1.call-start = ((), (), s32[]{:S(2)}) async-start(), calls=%async_computation.7 | async-start | bytes 1572864 | tf_op jit(solution)/shard_map/reduce_scatter | solution.py:123
  105.1 48.3 %copy-start = (bf16[512,4096]{1,0:T(8,128)(2,1)S(1)}, bf16[512,4096]{1,0:T(8,128)(2,1)}, u32[]{:S(2)}) copy-start(bf16[512,4096]{1,0:T(8,128)(2,1)} %param.11) | copy-start | bytes 12582916
  105.1 48.3 %copy-start.1 = (bf16[128,512]{1,0:T(8,128)(2,1)S(1)}, bf16[128,512]{1,0:T(8,128)(2,1)}, u32[]{:S(2)}) copy-start(bf16[128,512]{1,0:T(8,128)(2,1)} %param.8) | copy-start | bytes 393220
  105.1 48.3 %copy-start.2 = (bf16[128,512]{1,0:T(8,128)(2,1)S(1)}, bf16[128,512]{1,0:T(8,128)(2,1)}, u32[]{:S(2)}) copy-start(bf16[128,512]{1,0:T(8,128)(2,1)} %param.7) | copy-start | bytes 393220
  105.1 48.3 %copy-start.3 = (bf16[128,512]{1,0:T(8,128)(2,1)S(1)}, bf16[128,512]{1,0:T(8,128)(2,1)}, u32[]{:S(2)}) copy-start(bf16[128,512]{1,0:T(8,128)(2,1)} %param.6) | copy-start | bytes 393220
  105.1 48.3 %copy-start.4 = (f32[512]{0:T(512)S(1)}, f32[512]{0:T(512)}, u32[]{:S(2)}) copy-start(f32[512]{0:T(512)} %param.10) | copy-start | bytes 6148
Sparse Core Ops, SparseCore 0:
  155.3 18.6 reduce-scatter.1
